TPU v7x, 256 devices: a whole 4x4x8 slice. The times are simulated.
256 devices in a mesh: ctx: 64 (over y_lo, z, x), wt: 4 (over y_hi, core).
Axes of the slice: x: 4, y: 4 (y_hi: 2, y_lo: 2; y = y_hi * 2 + y_lo), z: 8, core: 2. Of those that a mesh axis runs over, the one named last changes fastest.
Arguments:
- tokens: bfloat16 [32768, 4096], P('ctx'), may hold values from -6 to 6
- round_var: float32 [4096, 4096], P('ctx', 'wt'), may hold values from -6 to 6
- grid_base: bfloat16 [4096, 4096], P('ctx', 'wt'), may hold values from -8 to 7, as said below
- col_scale: float32 [4096], P('wt'), may hold values from 0.0015 to 0.006
- queries: bfloat16 [32768, 4096], P('ctx', 'wt'), may hold values from -4 to 4
- keys: bfloat16 [32768, 4096], P('ctx', 'wt'), may hold values from -4 to 4
- gates: bfloat16 [32768, 4096], P('ctx', 'wt'), may hold values from -6 to 6
- target: bfloat16 [32768, 4096], P('ctx', 'wt'), may hold values from -6 to 6
- decay_code: int32 [32], P('wt'), may hold values from 7 to 19
- boundary: int32 [128], P('ctx'), may hold values from 0 to 1, as said below
Outputs:
- gated_out: bfloat16 [32768, 4096], P('ctx', 'wt')
- rounding_grad: float32 [4096, 4096], P('ctx', 'wt')
Inputs may be any that keep to these rules, and one draw needn't show every extreme that they name: `grid_base`: integer grid levels. At least one group begins after a segment boundary.
All inputs are finite; a program needn't handle non-finite values.
Results may differ from a plain program's by a relative error of at most 0.011.
Values may be sent and summed in bfloat16 or wider, within the bound.
A program may use at most 128 MiB of HBM per device.

v0:
```python
import math
import jax
import jax.numpy as jnp
from jax import lax
from jax.sharding import PartitionSpec as P

HEADS = 32
HEAD = 128
GROUP = 256
epsilon = 1e-06
loss_weight = 1024.0


def carried_in(part, axis, combine, identity, reverse):
    count = lax.axis_size(axis)
    place = lax.axis_index(axis)
    ahead = count - 1 - place if reverse else place
    gathered = jax.tree.map(lambda a: lax.all_gather(a, axis), part)
    state = jax.tree.map(lambda a, e: jnp.zeros_like(a) + jnp.asarray(e, a.dtype), part, identity)

    def one(step, state):
        source = count - 1 - step if reverse else step
        return combine(
            state, jax.tree.map(lambda a: lax.dynamic_index_in_dim(a, source, 0, False), gathered)
        )

    return lax.fori_loop(0, ahead, one, state)


def combine(earlier, later):
    return (earlier[0] * later[0], later[0][:, None, None] * earlier[1] + later[1])


def tables(decay_code):
    decay_rate = jnp.exp2(-decay_code.astype(jnp.float32))
    offsets = jnp.arange(GROUP).astype(jnp.float32)
    query_decay = jnp.exp(-offsets[:, None] * decay_rate[None, :])
    key_decay = jnp.exp(-(GROUP - offsets)[:, None] * decay_rate[None, :])
    spacing = offsets[:, None] - offsets[None, :]
    causal_decay = jnp.where(
        spacing[None] >= 0.0,
        jnp.exp(-jnp.maximum(spacing, 0.0)[None] * decay_rate[:, None, None]),
        0.0,
    )
    group_decay = jnp.exp(-GROUP * decay_rate)
    return (query_decay, key_decay, causal_decay, group_decay)


def on_device(
    tokens, round_var, grid_base, col_scale, queries, keys, gates, target, decay_code, boundary
):
    squash = jax.nn.sigmoid(round_var)
    raw_level = 1.2 * squash - 0.1
    soft_part = jnp.clip(raw_level, 0.0, 1.0)
    slopes = jnp.where((raw_level > 0.0) & (raw_level < 1.0), 1.2 * squash * (1.0 - squash), 0.0)
    weight = (col_scale[None, :] * (grid_base.astype(jnp.float32) + soft_part)).astype(jnp.bfloat16)
    rows_here = tokens.shape[0]
    col_count = queries.shape[1]
    head_count = col_count // HEAD
    blocks = rows_here // GROUP
    ctx_count = lax.axis_size("ctx")
    projected = jnp.dot(
        tokens,
        lax.all_gather(weight, "ctx", axis=0, tiled=True),
        preferred_element_type=jnp.float32,
    )
    shape4 = (blocks, GROUP, head_count, HEAD)
    value_all = projected.astype(jnp.bfloat16).reshape(shape4)
    query_all = queries.reshape(shape4)
    key_all = keys.reshape(shape4)
    query_decay, key_decay, causal_decay, group_decay = tables(decay_code)
    scores = jnp.einsum("cihd,cjhd->chij", query_all, key_all, preferred_element_type=jnp.float32)
    weights = (scores * causal_decay[None]).astype(jnp.bfloat16)
    query_dec = (query_all * query_decay[None, :, :, None]).astype(jnp.bfloat16)
    key_dec = (key_all * key_decay[None, :, :, None]).astype(jnp.bfloat16)
    intra = jnp.einsum("chij,cjhe->cihe", weights, value_all, preferred_element_type=jnp.float32)
    updates = jnp.einsum("cjhd,cjhe->chde", key_dec, value_all, preferred_element_type=jnp.float32)
    multiplier = 1.0 - 0.5 * boundary.astype(jnp.float32)
    local_state = jnp.zeros((head_count, HEAD, HEAD), jnp.float32)
    state_coef = jnp.ones((head_count,), jnp.float32)
    local_list = []
    coef_list = []
    for block in range(blocks):
        state_coef = state_coef * multiplier[block]
        local_state = multiplier[block] * local_state
        local_list.append(local_state)
        coef_list.append(state_coef)
        local_state = group_decay[:, None, None] * local_state + updates[block]
        state_coef = state_coef * group_decay
    prefix = carried_in(
        (state_coef, local_state),
        "ctx",
        combine,
        (jnp.ones_like(state_coef), jnp.zeros_like(local_state)),
        False,
    )
    entering = prefix[1]
    states = jnp.stack(
        [
            part_state + part_coef[:, None, None] * entering
            for part_state, part_coef in zip(local_list, coef_list)
        ]
    )
    attn_all = intra + jnp.einsum(
        "cihd,chde->cihe",
        query_dec,
        states.astype(jnp.bfloat16),
        preferred_element_type=jnp.float32,
    )
    attn = attn_all.reshape(rows_here, col_count)
    row_squares = lax.psum(jnp.sum(attn * attn, axis=1), "wt")
    rms = jnp.sqrt(row_squares / (HEADS * HEAD) + epsilon)
    normed = attn / rms[:, None]
    gate_open = jax.nn.sigmoid(gates.astype(jnp.float32))
    gated = normed * gate_open
    gated_out = gated.astype(jnp.bfloat16)
    grad_gated = (gated - target.astype(jnp.float32)) * (
        loss_weight / math.sqrt(rows_here * ctx_count)
    )
    grad_normed = grad_gated * gate_open
    row_inner = lax.psum(jnp.sum(grad_normed * normed, axis=1), "wt")
    grad_attn = (
        (grad_normed - normed * (row_inner / (HEADS * HEAD))[:, None]) / rms[:, None]
    ).astype(jnp.bfloat16)
    grad_all = grad_attn.reshape(shape4)
    back_intra = jnp.einsum(
        "chij,cihe->cjhe", weights, grad_all, preferred_element_type=jnp.float32
    )
    collected = jnp.einsum(
        "cihd,cihe->chde", query_dec, grad_all, preferred_element_type=jnp.float32
    )
    later_local = jnp.zeros((head_count, HEAD, HEAD), jnp.float32)
    later_coef = jnp.ones((head_count,), jnp.float32)
    next_list = [None] * blocks
    next_coefs = [None] * blocks
    for block in reversed(range(blocks)):
        next_list[block] = later_local
        next_coefs[block] = later_coef
        later_local = multiplier[block] * (
            collected[block] + group_decay[:, None, None] * later_local
        )
        later_coef = later_coef * group_decay * multiplier[block]
    suffix = carried_in(
        (later_coef, later_local),
        "ctx",
        combine,
        (jnp.ones_like(later_coef), jnp.zeros_like(later_local)),
        True,
    )
    from_later = suffix[1]
    next_states = jnp.stack(
        [
            part_state + part_coef[:, None, None] * from_later
            for part_state, part_coef in zip(next_list, next_coefs)
        ]
    )
    grad_values = back_intra + jnp.einsum(
        "cjhd,chde->cjhe",
        key_dec,
        next_states.astype(jnp.bfloat16),
        preferred_element_type=jnp.float32,
    )
    grad_values = grad_values.astype(jnp.bfloat16).reshape(rows_here, col_count)
    full_term = lax.dot_general(
        tokens, grad_values, (((0,), (0,)), ((), ())), preferred_element_type=jnp.float32
    )
    weight_grad = lax.psum_scatter(full_term, "ctx", scatter_dimension=0, tiled=True)
    rounding_grad = col_scale[None, :] * slopes * weight_grad
    return (gated_out, rounding_grad)


def solution(mesh):
    placed = (
        P("ctx", None),
        P("ctx", "wt"),
        P("ctx", "wt"),
        P("wt"),
        P("ctx", "wt"),
        P("ctx", "wt"),
        P("ctx", "wt"),
        P("ctx", "wt"),
        P("wt"),
        P("ctx"),
    )
    return jax.shard_map(
        on_device,
        mesh=mesh,
        in_specs=placed,
        out_specs=(P("ctx", "wt"), P("ctx", "wt")),
        check_vma=False,
    )
```

profile of v0, /device:TPU:24, one launch (start us, length us, event | category | flops | bytes accessed | tf_op | source)
XLA Modules:
  0.0 1666.2 jit_solution(1325036017043877112)
XLA Ops:
  7.2 1.8 multiply_convert_fusion.7
  15.1 307.1 %all-gather.6.cloned.1.call-done = bf16[4096,1024]{1,0:T(8,128)(2,1)} async-done(((bf16[64,1024]{1,0:T(8,128)(2,1)}), bf16[4096,1024]{1,0:T(8,128)(2,1)}) %all-gather.6.cloned.1.call-update) | async-done | bytes 8388624 | tf_op jit(solution)/shard_map/all_gather | solution.py:64
  322.2 9.1 fusion
  336.7 160.3 %all-reduce.2 = (f32[512]{0:T(512)S(1)}, f32[512]{0:T(512)S(1)}) all-reduce(f32[512]{0:T(512)S(1)} %get-tuple-element.170, f32[512]{0:T(512)S(1)} %multiply_dynamic-update-slice_fusion), channel_id=2, replica_groups=mesh['ctx'=64,'wt'=4] {'ctx'}, use_global_device_ids=true, to_apply=%add | all-reduce | flops 1024 | bytes 8192
  497.1 1.5 copy.65
  502.6 2.1 fusion.34
  504.7 208.0 %all-gather.8.cloned.1.call-done = f32[64,8,128,128]{3,2,1,0:T(8,128)} async-done(((f32[1,8,128,128]{3,2,1,0:T(8,128)}), f32[64,8,128,128]{3,2,1,0:T(8,128)}) %all-gather.8.cloned.1.call-update) | async-done | bytes 33554448 | tf_op jit(solution)/shard_map/all_gather | solution.py:18
  712.8 39.4 %while.26 = (s32[]{:T(128)}, f32[8,128,128]{2,1,0:T(8,128)S(1)}, s32[]{:T(128)}, f32[64,8]{1,0:T(8,128)S(1)}, f32[64,8,128,128]{3,2,1,0:T(8,128)}, /*index=5*/s32[]{:T(128)}, s32[]{:T(128)}, s32[]{:T(128)}) while((s32[]{:T(128)}, f32[8,128,128]{2,1,0:T(8,128)S(1)}, s32[]{:T(128)}, f32[64,8]{1,0:T(8,128)S(1)}, f32[64,8,128,128]{3,2,1,0:T(8,128)}, ...), condition=%wide.region_1.2_spmd, body=%wide.region_0.1_spmd.sunk | while | flops 262149 | bytes 1573095 | solution.py:27
  752.2 2.5 fusion.27
  754.7 3.5 multiply_reduce_fusion.1
  758.1 7.1 psum.14
  765.3 3.0 copy.53
  768.3 3.0 multiply_reduce_fusion
  771.3 8.2 psum.15
  779.5 4.1 fusion.4
  786.3 2.1 fusion.12
  788.6 1.8 fusion.6
  790.4 406.6 %all-gather.10.cloned.1.call-done = f32[64,8,128,128]{3,2,1,0:T(8,128)} async-done(((f32[1,8,128,128]{3,2,1,0:T(8,128)}), f32[64,8,128,128]{3,2,1,0:T(8,128)}) %all-gather.10.cloned.1.call-update) | async-done | bytes 33554448 | tf_op jit(solution)/shard_map/all_gather | solution.py:18
  1197.0 38.3 %while.27 = (s32[]{:T(128)}, f32[8,128,128]{2,1,0:T(8,128)S(1)}, s32[]{:T(128)}, f32[64,8]{1,0:T(8,128)S(1)}, f32[64,8,128,128]{3,2,1,0:T(8,128)}, /*index=5*/s32[]{:T(128)}, s32[]{:T(128)}, s32[]{:T(128)}, s32[]{:T(128)}) while((s32[]{:T(128)}, f32[8,128,128]{2,1,0:T(8,128)S(1)}, s32[]{:T(128)}, f32[64,8]{1,0:T(8,128)S(1)}, ...), condition=%wide.region_7.8_spmd, body=%wide.region_6.7_spmd.sunk | while | flops 262150 | bytes 1573115 | solution.py:27
  1235.4 1.9 fusion.29
  1238.8 10.4 convolution_bitcast_fusion
  1249.2 17.4 %copy.63 = f32[4096,1024]{1,0:T(8,128)} copy(f32[4096,1024]{0,1:T(8,128)} %convolution_bitcast_fusion) | data formatting | bytes 33554432
  1266.7 391.2 %reduce-scatter.4.cloned.1.call-done = f32[64,1024]{1,0:T(8,128)} async-done(((f32[4096,1024]{1,0:T(8,128)}), f32[64,1024]{1,0:T(8,128)}) %reduce-scatter.4.cloned.1.call-update) | async-done | bytes 262160 | tf_op jit(solution)/shard_map/reduce_scatter | solution.py:167
  1657.9 1.8 multiply_multiply_fusion.1
  (198 shorter events, 94.3 us)
Async XLA Ops:
  7.2 3.5 copy-start.15
  7.2 4.8 copy-start.14
  7.2 6.0 copy-start.13
  7.2 315.0 %all-gather.6.cloned.1.call-start = ((), (), s32[]{:S(2)}) async-start(), calls=%async_computation.1 | async-start | bytes 8519680 | tf_op jit(solution)/shard_map/all_gather | solution.py:64
  9.1 703.7 %all-gather.8.cloned.1.call-start = ((), (), s32[]{:S(2)}) async-start(), calls=%async_computation.2 | async-start | bytes 34078720 | tf_op jit(solution)/shard_map/all_gather | solution.py:18
  10.6 490.1 %copy-start = (bf16[64,8,8,128]{3,2,1,0:T(8,128)(2,1)}, bf16[64,8,8,128]{3,2,1,0:T(8,128)(2,1)S(1)}, u32[]{:S(2)}) copy-start(bf16[64,8,8,128]{3,2,1,0:T(8,128)(2,1)S(1)} %copy.66) | copy-start | bytes 3145732
  332.6 2.8 copy-start.5
  333.9 164.8 %copy-start.8 = (f32[2,8,128,128]{3,2,1,0:T(8,128)}, f32[2,8,128,128]{3,2,1,0:T(8,128)S(1)}, u32[]{:S(2)}) copy-start(f32[2,8,128,128]{3,2,1,0:T(8,128)S(1)} %fusion.11) | copy-start | bytes 3145732
  335.4 861.6 %all-gather.10.cloned.1.call-start = ((), (), s32[]{:S(2)}) async-start(), calls=%async_computation.3 | async-start | bytes 34078720 | tf_op jit(solution)/shard_map/all_gather | solution.py:18
  500.1 1.2 copy-start.2
  501.4 1.2 copy-start.6
  752.2 2.5 copy-start.3
  765.3 3.0 copy-start.10
  783.6 1.2 copy-start.4
  785.3 1.0 copy-start.9
  788.4 869.5 %reduce-scatter.4.cloned.1.call-start = ((), (), s32[]{:S(2)}) async-start(), calls=%async_computation.4 | async-start | bytes 17039360 | tf_op jit(solution)/shard_map/reduce_scatter | solution.py:167
  1197.0 40.2 %copy-start.7 = (f32[2,8,128,256]{3,2,1,0:T(8,128)S(1)}, f32[2,8,128,256]{3,2,1,0:T(8,128)}, u32[]{:S(2)}) copy-start(f32[2,8,128,256]{3,2,1,0:T(8,128)} %fusion.6) | copy-start | bytes 6291460
  1235.4 1.9 copy-start.1
  1266.6 391.3 %copy-start.11 = (f32[64,1024]{1,0:T(8,128)S(1)}, f32[64,1024]{1,0:T(8,128)}, u32[]{:S(2)}) copy-start(f32[64,1024]{1,0:T(8,128)} %param.15) | copy-start | bytes 786436
  1266.6 391.3 %copy-start.12 = (f32[1024]{0:T(1024)S(1)}, f32[1024]{0:T(1024)}, u32[]{:S(2)}) copy-start(f32[1024]{0:T(1024)} %param.17) | copy-start | bytes 12292
Sparse Core Ops, SparseCore 0:
  10.4 311.8 all-gather.5
  335.5 377.1 all-gather.7
  788.6 408.3 all-gather.9
  1266.8 391.0 reduce-scatter.3
where the time goes:
time: 1670 us
  waiting for transfers between devices  1310 us (78%)
  blocking collectives  176 us (11%)
  other arithmetic  97.5 us (6%)
  local copies, waits for them, and re-layouts  32.3 us (2%)
  matrix products  30.2 us (2%)
    all_gather x2, waiting for transfers between devices, carried_in(): gathered = jax.tree.map(lambda a: lax.all_gather(a, axis), part)  615 us
    reduce_scatter x1, waiting for transfers between devices, on_device(): lax.psum_scatter(full_term, 'ctx', scatter_dimension=0, tiled=True)  391 us
    all_gather x1, waiting for transfers between devices, on_device(): lax.all_gather(weight, 'ctx', axis=0, tiled=True)  307 us
    unnamed x1, blocking collectives  160 us
    add x63, other arithmetic, combine(): later[0][:, None, None] * earlier[1] + later[1]  75.1 us
  transfers between devices with their start and end apart: 4, of which 4 were waited for; matrix products, arithmetic and copies ran while one was open for 1% of the time, Pallas kernels for 0%

commit v1 on v0

--- a/solution.py
+++ b/solution.py
@@ -1,3 +1,4 @@
+import functools
 import math
 import jax
 import jax.numpy as jnp
@@ -9,6 +10,21 @@
 GROUP = 256
 epsilon = 1e-06
 loss_weight = 1024.0
+
+
+def wait_fields(message, which_axis):
+    return jnp.concatenate(
+        lax.all_to_all(
+            jnp.stack([message for _ in range(lax.psum(1, axis_name=which_axis))]),
+            axis_name=which_axis,
+            split_axis=0,
+            concat_axis=0,
+        ),
+        axis=0,
+    )
+
+
+_balance_types = functools.partial(wait_fields, which_axis="ctx")
 
 
 def carried_in(part, axis, combine, identity, reverse):
@@ -59,11 +75,7 @@
     head_count = col_count // HEAD
     blocks = rows_here // GROUP
     ctx_count = lax.axis_size("ctx")
-    projected = jnp.dot(
-        tokens,
-        lax.all_gather(weight, "ctx", axis=0, tiled=True),
-        preferred_element_type=jnp.float32,
-    )
+    projected = jnp.dot(tokens, _balance_types(weight), preferred_element_type=jnp.float32)
     shape4 = (blocks, GROUP, head_count, HEAD)
     value_all = projected.astype(jnp.bfloat16).reshape(shape4)
     query_all = queries.reshape(shape4)

time: 1670 us -> 1560 us (0.934)
  waiting for transfers between devices: 1310 us -> 1180 us
    reduce_scatter x1 -> x0, waiting for transfers between devices: 391 us -> none  [on_device(): lax.psum_scatter(full_term, 'ctx', scatter_dimension=0, tiled=True)]
    unnamed x4, waiting for transfers between devices: 0.07 us -> 391 us
    all_gather x1 -> x0, waiting for transfers between devices: 307 us -> none  [on_device(): lax.all_gather(weight, 'ctx', axis=0, tiled=True)]
    all_to_all x0 -> x1, waiting for transfers between devices: none -> 178 us  [wait_fields(): lax.all_to_all(jnp.stack([message for _ in range(lax.psum(1, axis_name=wh...]
where the time goes in v1:
time: 1560 us
  waiting for transfers between devices  1180 us (76%)
  blocking collectives  176 us (11%)
  other arithmetic  95.9 us (6%)
  local copies, waits for them, and re-layouts  40.3 us (3%)
  matrix products  30.2 us (2%)
    all_gather x2, waiting for transfers between devices, carried_in(): gathered = jax.tree.map(lambda a: lax.all_gather(a, axis), part)  615 us
    unnamed x4, waiting for transfers between devices  391 us
    all_to_all x1, waiting for transfers between devices, wait_fields(): lax.all_to_all(jnp.stack([message for _ in range(lax.psum(1, axis_name=wh...  178 us
    unnamed x1, blocking collectives  161 us
    add x63, other arithmetic, combine(): later[0][:, None, None] * earlier[1] + later[1]  75.1 us
  transfers between devices with their start and end apart: 4, of which 4 were waited for; matrix products, arithmetic and copies ran while one was open for 1% of the time, Pallas kernels for 0%

profile of v1, /device:TPU:24, one launch (start us, length us, event | category | flops | bytes accessed | tf_op | source)
XLA Modules:
  0.0 1558.1 jit_solution(3448030889412618580)
XLA Ops:
  10.6 4.3 stack.20
  14.9 13.4 all-to-all-start
  33.7 177.7 %all-to-all-done = bf16[64,64,1024]{2,1,0:T(8,128)(2,1)} async-done(((bf16[64,64,1024]{2,1,0:T(8,128)(2,1)}), bf16[64,64,1024]{2,1,0:T(8,128)(2,1)}, u32[]{:S(2)}, u32[]{:S(2)}) %all-to-all-start) | async-done | bytes 8388640 | tf_op jit(solution)/shard_map/all_to_all | solution.py:17
  211.4 9.1 fusion
  223.0 1.6 slice_add_fusion.1
  226.0 161.1 %all-reduce.2 = (f32[512]{0:T(512)S(1)}, f32[512]{0:T(512)S(1)}) all-reduce(f32[512]{0:T(512)S(1)} %get-tuple-element.172, f32[512]{0:T(512)S(1)} %multiply_dynamic-update-slice_fusion), channel_id=2, replica_groups=mesh['ctx'=64,'wt'=4] {'ctx'}, use_global_device_ids=true, to_apply=%add | all-reduce | flops 1024 | bytes 8192
  392.7 2.1 fusion.34
  394.8 208.4 %all-gather.5.cloned.1.call-done = f32[64,8,128,128]{3,2,1,0:T(8,128)} async-done(((f32[1,8,128,128]{3,2,1,0:T(8,128)}), f32[64,8,128,128]{3,2,1,0:T(8,128)}) %all-gather.5.cloned.1.call-update) | async-done | bytes 33554448 | tf_op jit(solution)/shard_map/all_gather | solution.py:34
  603.3 39.7 %while.26 = (s32[]{:T(128)}, f32[8,128,128]{2,1,0:T(8,128)S(1)}, s32[]{:T(128)}, f32[64,8]{1,0:T(8,128)S(1)}, f32[64,8,128,128]{3,2,1,0:T(8,128)}, /*index=5*/s32[]{:T(128)}, s32[]{:T(128)}, s32[]{:T(128)}) while((s32[]{:T(128)}, f32[8,128,128]{2,1,0:T(8,128)S(1)}, s32[]{:T(128)}, f32[64,8]{1,0:T(8,128)S(1)}, f32[64,8,128,128]{3,2,1,0:T(8,128)}, ...), condition=%wide.region_1.2_spmd, body=%wide.region_0.1_spmd.sunk | while | flops 262149 | bytes 1573087 | solution.py:43
  643.0 2.6 fusion.27
  645.6 3.5 multiply_reduce_fusion.1
  649.1 3.0 copy.58
  652.1 7.1 psum.14
  659.2 3.0 multiply_reduce_fusion
  662.2 8.0 psum.15
  670.2 4.1 fusion.4
  677.0 2.2 fusion.12
  679.4 1.8 fusion.6
  681.3 406.8 %all-gather.7.cloned.1.call-done = f32[64,8,128,128]{3,2,1,0:T(8,128)} async-done(((f32[1,8,128,128]{3,2,1,0:T(8,128)}), f32[64,8,128,128]{3,2,1,0:T(8,128)}) %all-gather.7.cloned.1.call-update) | async-done | bytes 33554448 | tf_op jit(solution)/shard_map/all_gather | solution.py:34
  1088.1 38.5 %while.27 = (s32[]{:T(128)}, f32[8,128,128]{2,1,0:T(8,128)S(1)}, s32[]{:T(128)}, f32[64,8]{1,0:T(8,128)S(1)}, f32[64,8,128,128]{3,2,1,0:T(8,128)}, /*index=5*/s32[]{:T(128)}, s32[]{:T(128)}, s32[]{:T(128)}, s32[]{:T(128)}) while((s32[]{:T(128)}, f32[8,128,128]{2,1,0:T(8,128)S(1)}, s32[]{:T(128)}, f32[64,8]{1,0:T(8,128)S(1)}, ...), condition=%wide.region_7.8_spmd, body=%wide.region_6.7_spmd.sunk | while | flops 262150 | bytes 1573107 | solution.py:43
  1126.7 2.0 fusion.29
  1130.2 10.4 convolution_bitcast_fusion
  1140.6 17.4 %copy.68 = f32[4096,1024]{1,0:T(8,128)} copy(f32[4096,1024]{0,1:T(8,128)} %convolution_bitcast_fusion) | data formatting | bytes 33554432
  1158.1 391.2 %reduce-scatter.4.cloned.1.call-done = f32[64,1024]{1,0:T(8,128)} async-done(((f32[4096,1024]{1,0:T(8,128)}), f32[64,1024]{1,0:T(8,128)}) %reduce-scatter.4.cloned.1.call-update) | async-done | bytes 262160
  (207 shorter events, 99.5 us)
Async XLA Ops:
  8.3 6.6 copy-start.10
  14.9 13.5 copy-start.13
  14.9 196.5 %all-to-all-start = ((bf16[64,64,1024]{2,1,0:T(8,128)(2,1)}), bf16[64,64,1024]{2,1,0:T(8,128)(2,1)}, u32[]{:S(2)}, u32[]{:S(2)}) async-start(bf16[64,64,1024]{2,1,0:T(8,128)(2,1)} %stack.20), calls=%async_computation | async-start | bytes 16777216 | tf_op jit(solution)/shard_map/all_to_all | solution.py:17
  28.3 0.7 copy-start.16
  28.3 2.0 copy-start.17
  28.3 3.3 copy-start.15
  28.3 574.9 %all-gather.5.cloned.1.call-start = ((), (), s32[]{:S(2)}) async-start(), calls=%async_computation.2 | async-start | bytes 34078720 | tf_op jit(solution)/shard_map/all_gather | solution.py:34
  28.9 361.9 %copy-start = (bf16[64,8,8,128]{3,2,1,0:T(8,128)(2,1)}, bf16[64,8,8,128]{3,2,1,0:T(8,128)(2,1)S(1)}, u32[]{:S(2)}) copy-start(bf16[64,8,8,128]{3,2,1,0:T(8,128)(2,1)S(1)} %copy.71) | copy-start | bytes 3145732
  221.7 2.9 copy-start.5
  223.0 165.7 %copy-start.8 = (f32[2,8,128,128]{3,2,1,0:T(8,128)}, f32[2,8,128,128]{3,2,1,0:T(8,128)S(1)}, u32[]{:S(2)}) copy-start(f32[2,8,128,128]{3,2,1,0:T(8,128)S(1)} %fusion.11) | copy-start | bytes 3145732
  224.6 863.5 %all-gather.7.cloned.1.call-start = ((), (), s32[]{:S(2)}) async-start(), calls=%async_computation.3 | async-start | bytes 34078720 | tf_op jit(solution)/shard_map/all_gather | solution.py:34
  390.2 1.2 copy-start.2
  391.4 1.2 copy-start.6
  643.0 2.6 copy-start.3
  649.1 10.1 copy-start.12
  674.3 1.2 copy-start.4
  676.0 1.0 copy-start.9
  679.3 870.0 %reduce-scatter.4.cloned.1.call-start = ((), (), s32[]{:S(2)}) async-start(), calls=%async_computation.4 | async-start | bytes 17039360
  1088.1 40.5 %copy-start.7 = (f32[2,8,128,256]{3,2,1,0:T(8,128)S(1)}, f32[2,8,128,256]{3,2,1,0:T(8,128)}, u32[]{:S(2)}) copy-start(f32[2,8,128,256]{3,2,1,0:T(8,128)} %fusion.6) | copy-start | bytes 6291460
  1126.7 2.0 copy-start.1
  1158.0 392.4 %copy-start.11 = (f32[64,1024]{0,1:T(8,128)S(1)}, f32[64,1024]{0,1:T(8,128)}, u32[]{:S(2)}) copy-start(f32[64,1024]{0,1:T(8,128)} %copy-done.10) | copy-start | bytes 786436
  1158.0 392.4 %copy-start.14 = (f32[1024]{0:T(1024)S(1)}, f32[1024]{0:T(1024)}, u32[]{:S(2)}) copy-start(f32[1024]{0:T(1024)} %param.17) | copy-start | bytes 12292
Sparse Core Ops, SparseCore 0:
  224.7 378.4 all-gather.4
  679.4 408.6 all-gather.6
  1158.2 391.0 reduce-scatter.3
